TPU v7x, 32 devices: a whole 2x2x4 slice. The times are simulated.
32 devices in a mesh: ex: 4 (over z), col: 4 (over y, core), lay: 2 (over x).
Axes of the slice: x: 2, y: 2, z: 4, core: 2. Of those that a mesh axis runs over, the one named last changes fastest.
Arguments:
- normalized: bfloat16 [256, 2, 4, 3584], P('ex', 'lay', None, 'col'), may hold values from -6 to 6
- upstream: bfloat16 [256, 2, 4, 3584], P('ex', 'lay', None, 'col'), may hold values from -3 to 3
- owner_order: int32 [4, 64], P('ex'), may hold values from 0 to 63, each once within a row
- sketch_index: int32 [2, 28, 4], P(None, 'col'), may hold values from 0 to 63, all different within a row
- sketch_scale: bfloat16 [2, 28, 4], P(None, 'col'), may hold values from -1.5 to 1.5
- query_sketch: bfloat16 [4, 8192], P('ex', 'col'), may hold values from -0.0625 to 0.0625
Outputs:
- sketch: bfloat16 [256, 8192], P(('ex', 'lay'), 'col')
- scores: float32 [256, 4], P(('ex', 'lay'), 'col')
Inputs may be any that keep to these rules, and one draw needn't show every extreme that they name: Each row is an ordering of the 64 examples of one block; the example at place j of row g is training example g * 64 + owner_order[g, j]. `sketch_index`: the 4 output blocks of one input block are distinct; every output block is named by some input block.
All inputs are finite; a program needn't handle non-finite values.
Results may differ from a plain program's by a relative error of at most 0.0049.
Values may be sent and summed in bfloat16 or wider, within the bound.
A program may use at most 64 MiB of HBM per device.

v0:
```python
import math

import jax
import jax.numpy as jnp
from jax import lax
from jax.sharding import PartitionSpec as P

SKETCH = 8192


def hadamard_table():
    counter = jnp.arange(128, dtype=jnp.int32)
    both = counter[:, None] & counter[None, :]
    parity = jnp.zeros((128, 128), jnp.int32)
    for shift_bit in range(7):
        parity = parity + (both >> shift_bit & 1)
    signs = 1 - 2 * (parity % 2)
    return signs.astype(jnp.float32) / math.sqrt(128.0)


def build_table(sketch_index, sketch_scale, out_blocks):
    targets = jnp.arange(out_blocks, dtype=jnp.int32)
    table = (sketch_index[..., None] == targets).astype(jnp.float32) * sketch_scale.astype(
        jnp.float32
    )[..., None]
    return jnp.sum(table, axis=2).reshape(-1, out_blocks)


def local(normalized, upstream, owner_order, sketch_index, sketch_scale, query_sketch):
    local_grads = jnp.sum(
        normalized.astype(jnp.float32) * upstream.astype(jnp.float32), axis=2
    ).astype(jnp.bfloat16)
    reordered = jnp.take(local_grads, owner_order[0], axis=0)
    owned = lax.all_to_all(reordered, "lay", split_axis=0, concat_axis=1, tiled=True)
    own_rows = owned.shape[0]
    out_blocks = SKETCH // 128
    full_rows, full_index, full_scale = (
        lax.all_gather(owned, "col", axis=2, tiled=True),
        lax.all_gather(sketch_index, "col", axis=1, tiled=True),
        lax.all_gather(sketch_scale, "col", axis=1, tiled=True),
    )
    layer_count, feature_width = (full_rows.shape[1], full_rows.shape[2])
    table = build_table(full_index, full_scale, out_blocks)
    my_blocks = out_blocks // lax.axis_size("col")
    my_table = lax.dynamic_slice_in_dim(table, lax.axis_index("col") * my_blocks, my_blocks, 1)
    grad_rows = full_rows.reshape(own_rows, layer_count * (feature_width // 128), 128).astype(
        jnp.float32
    )
    summed = jnp.einsum("ebc,bo->eoc", grad_rows, my_table, precision=lax.Precision.HIGHEST)
    rotated = jnp.einsum("eoc,cd->eod", summed, hadamard_table(), precision=lax.Precision.HIGHEST)
    sketch = rotated.reshape(own_rows, -1).astype(jnp.bfloat16)
    partial_scores = jnp.einsum(
        "ec,qc->eq",
        sketch,
        lax.all_gather(query_sketch, "ex", axis=0, tiled=True),
        preferred_element_type=jnp.float32,
    )
    scores = lax.psum_scatter(partial_scores, "col", scatter_dimension=1, tiled=True)
    return (sketch, scores)


def solution(mesh):
    placed = (
        P("ex", "lay", None, "col"),
        P("ex", "lay", None, "col"),
        P("ex", None),
        P(None, "col", None),
        P(None, "col", None),
        P("ex", "col"),
    )
    return jax.shard_map(
        local,
        mesh=mesh,
        in_specs=placed,
        out_specs=(P(("ex", "lay"), "col"), P(("ex", "lay"), "col")),
        check_vma=False,
    )
```

profile of v0, /device:TPU:0, one launch (start us, length us, event | category | flops | bytes accessed | tf_op | source)
XLA Modules:
  0.0 53.9 jit_solution(2970445033246631568)
XLA Ops:
  0.6 0.0 copy-start.4
  0.6 0.7 %fusion.23 = s32[64]{0:T(128)S(1)} fusion(s32[1,64]{1,0:T(1,128)} %param.8), kind=kLoop, calls=%fused_computation.37 | loop fusion | flops 192 | bytes 512 | tf_op jit(solution)/shard_map/jit(_take)/jit(_where)/select_n | solution.py:33
  1.4 0.0 copy-done.4
  1.4 1.8 %multiply_reduce_fusion = bf16[64,896]{1,0:T(8,128)(2,1)S(1)} fusion(bf16[64,1,4,896]{3,2,1,0:T(4,128)(2,1)} %param.7, bf16[64,1,4,896]{3,2,1,0:T(4,128)(2,1)} %param.6), kind=kLoop, calls=%fused_computation.3 | loop fusion | flops 860160 | bytes 1032192 | tf_op jit(solution)/shard_map/reduce_sum | solution.py:30
  3.2 0.7 %gather_fusion = bf16[64,896]{1,0:T(8,128)(2,1)S(1)} fusion(bf16[64,896]{1,0:T(8,128)(2,1)S(1)} %multiply_reduce_fusion, s32[1024]{0:T(1024)S(1)} %pad_clamp_fusion), kind=kCustom, calls=%fused_computation | custom fusion | bytes 229632 | tf_op jit(solution)/shard_map/jit(_take)/gather | solution.py:33
  3.9 0.1 bitcast_select_fusion
  4.0 0.5 broadcast.80
  4.6 0.7 %reduce.1 = bf16[64,896]{1,0:T(8,128)(2,1)S(1)} reduce(bf16[64,1,896]{2,0,1:T(8,128)(2,1)S(1)} %bitcast_select_fusion, bf16[]{:T(256)} %broadcast.80), dimensions={1}, to_apply=%copy.40.reduce_sub_computation | reduce | bytes 229378 | tf_op jit(solution)/shard_map/jit(_take)/select_n | solution.py:33
  5.2 0.7 %reshape.102 = bf16[2,2,14336]{2,1,0:T(2,128)(2,1)} reshape(bf16[64,896]{1,0:T(8,128)(2,1)S(1)} %reduce.1) | data formatting | bytes 229376
  5.9 0.0 copy-start.3
  5.9 4.4 %all-to-all-start = ((bf16[2,2,14336]{2,1,0:T(2,128)(2,1)}), bf16[2,2,14336]{2,1,0:T(2,128)(2,1)S(1)}, u32[]{:S(2)}, u32[]{:S(2)}) async-start(bf16[2,2,14336]{2,1,0:T(2,128)(2,1)} %reshape.102), calls=%async_computation | async-start | bytes 229376 | tf_op jit(solution)/shard_map/all_to_all | solution.py:34
  10.3 0.0 copy-done.3
  10.3 0.1 copy.36
  10.4 5.4 %all_gather.13 = bf16[2,28,4]{2,0,1:T(2,128)(2,1)S(1)} all-gather(bf16[2,7,4]{2,0,1:T(2,128)(2,1)S(1)} %copy.36), channel_id=1, replica_groups=mesh['ex'=4,'col'=4,'lay'=2] {'col'}, dimensions={1}, use_global_device_ids=true | all-gather | bytes 560 | tf_op jit(solution)/shard_map/all_gather | solution.py:40
  15.8 0.1 copy.37
  15.9 0.0 copy-start.2
  15.9 0.1 copy.38
  16.0 0.6 %copy-done.2 = s32[2,7,4]{1,2,0:T(4,128)S(1)} copy-done((s32[2,7,4]{1,2,0:T(4,128)S(1)}, s32[2,7,4]{1,2,0:T(4,128)}, u32[]{:S(2)}) %copy-start.2) | copy-done | bytes 248
  16.6 0.1 copy.34
  16.7 5.4 %all_gather.12 = s32[2,28,4]{2,0,1:T(2,128)S(1)} all-gather(s32[2,7,4]{2,0,1:T(2,128)S(1)} %copy.34), channel_id=1, replica_groups=mesh['ex'=4,'col'=4,'lay'=2] {'col'}, dimensions={1}, use_global_device_ids=true | all-gather | bytes 1120 | tf_op jit(solution)/shard_map/all_gather | solution.py:39
  22.1 0.2 select_reduce_fusion
  22.3 0.0 copy-start.1
  22.4 0.0 copy-start.5
  22.4 0.6 %copy-done.5 = u32[32]{0:T(128)S(1)} copy-done((u32[32]{0:T(128)S(1)}, u32[32]{0:T(128)}, u32[]{:S(2)}) %copy-start.5) | copy-done | bytes 152
  23.0 0.7 %dynamic-slice = u32[1]{0:T(128)} dynamic-slice(u32[32]{0:T(128)S(1)} %copy-done.5, u32[]{:T(128)S(6)} %add.63), dynamic_slice_sizes={1} | dynamic-slice | bytes 12
  23.7 0.0 copy-done.1
  23.7 13.5 %all-gather.1 = bf16[4,1,2048]{2,1,0:T(2,128)(2,1)S(1)} all-gather(bf16[1,1,2048]{2,1,0:T(2,128)(2,1)S(1)} %bitcast.38), channel_id=1, replica_groups=mesh['ex'=4,'col'=4,'lay'=2] {'ex'}, dimensions={0}, use_global_device_ids=true | all-gather | bytes 20480 | tf_op jit(solution)/shard_map/all_gather | solution.py:55
  37.2 0.0 all-to-all-done
  37.2 0.1 reshape.103
  37.4 6.8 %all-gather = bf16[32,2,1,3584]{3,0,1,2:T(8,128)(2,1)S(1)} all-gather(bf16[32,2,1,896]{3,0,1,2:T(8,128)(2,1)S(1)} %bitcast.34), channel_id=2, replica_groups=mesh['ex'=4,'col'=4,'lay'=2] {'col'}, dimensions={3}, use_global_device_ids=true | all-gather | bytes 573440 | tf_op jit(solution)/shard_map/all_gather | solution.py:38
  44.2 0.5 copy.41
  44.7 0.3 reshape.83
  45.0 0.5 convolution_bitcast_fusion
  45.4 0.4 convolution_convert_fusion
  45.9 0.0 copy-start
  45.9 0.1 fusion.20
  46.1 6.6 %all-reduce = f32[32,4]{0,1:T(4,128)S(1)} all-reduce(f32[32,4]{0,1:T(4,128)S(1)} %fusion.20), channel_id=3, replica_groups=mesh['ex'=4,'col'=4,'lay'=2] {'col'}, use_global_device_ids=true, to_apply=%region_2.3.clone | all-reduce | flops 128 | bytes 1024
  52.7 1.2 %constant_dynamic-slice_fusion = f32[32,1]{0,1:T(1,128)} fusion(f32[32,4]{0,1:T(4,128)S(1)} %all-reduce, u32[]{:T(128)} %bitcast.9), kind=kLoop, calls=%fused_computation.38 | loop fusion | bytes 260
  53.9 0.0 copy-done
  (6 shorter events, 0.1 us)
Async XLA Ops:
  0.6 0.7 %copy-start.4 = (s32[1,64]{1,0:T(1,128)S(1)}, s32[1,64]{1,0:T(1,128)}, u32[]{:S(2)}) copy-start(s32[1,64]{1,0:T(1,128)} %param.8) | copy-start | bytes 772
  5.9 4.4 %copy-start.3 = (bf16[2,7,4]{1,2,0:T(4,128)(2,1)S(1)}, bf16[2,7,4]{1,2,0:T(4,128)(2,1)}, u32[]{:S(2)}) copy-start(bf16[2,7,4]{1,2,0:T(4,128)(2,1)} %param.10) | copy-start | bytes 340
  5.9 31.3 %all-to-all-start = ((bf16[2,2,14336]{2,1,0:T(2,128)(2,1)}), bf16[2,2,14336]{2,1,0:T(2,128)(2,1)S(1)}, u32[]{:S(2)}, u32[]{:S(2)}) async-start(bf16[2,2,14336]{2,1,0:T(2,128)(2,1)} %reshape.102), calls=%async_computation | async-start | bytes 229376 | tf_op jit(solution)/shard_map/all_to_all | solution.py:34
  15.9 0.7 %copy-start.2 = (s32[2,7,4]{1,2,0:T(4,128)S(1)}, s32[2,7,4]{1,2,0:T(4,128)}, u32[]{:S(2)}) copy-start(s32[2,7,4]{1,2,0:T(4,128)} %param.9) | copy-start | bytes 676
  22.3 1.3 %copy-start.1 = (bf16[1,2048]{1,0:T(2,128)(2,1)S(1)}, bf16[1,2048]{1,0:T(2,128)(2,1)}, u32[]{:S(2)}) copy-start(bf16[1,2048]{1,0:T(2,128)(2,1)} %param.11) | copy-start | bytes 12292
  22.4 0.7 %copy-start.5 = (u32[32]{0:T(128)S(1)}, u32[32]{0:T(128)}, u32[]{:S(2)}) copy-start(u32[32]{0:T(128)} %constant.65) | copy-start | bytes 388
  45.9 7.9 %copy-start = (bf16[4,8,16,128]{3,1,2,0:T(8,128)(2,1)}, bf16[4,8,16,128]{3,1,2,0:T(8,128)(2,1)S(1)}, u32[]{:S(2)}) copy-start(bf16[4,8,16,128]{3,1,2,0:T(8,128)(2,1)S(1)} %copy.51) | copy-start | bytes 393220
where the time goes:
time: 54.3 us; the launch traced here: 53.9 us
  blocking collectives  37.8 us (70%)
  local copies, waits for them, and re-layouts  6.38 us (12%)
  starting transfers between devices  4.37 us (8%)
  other arithmetic  3.53 us (7%)
  matrix products  1.03 us (2%)
  between operations  0.78 us (1%)
    all_gather x1, blocking collectives, local(): lax.all_gather(query_sketch, 'ex', axis=0, tiled=True)  13.5 us
    all_gather x1, blocking collectives, local(): lax.all_gather(owned, 'col', axis=2, tiled=True)  6.84 us
    unnamed x1, blocking collectives  6.58 us
    all_gather x1, blocking collectives, local(): lax.all_gather(sketch_index, 'col', axis=1, tiled=True)  5.43 us
    all_gather x1, blocking collectives, local(): lax.all_gather(sketch_scale, 'col', axis=1, tiled=True)  5.39 us
    all_to_all x1, starting transfers between devices, local(): lax.all_to_all(reordered, 'lay', split_axis=0, concat_axis=1, tiled=True)  4.37 us
    unnamed x20, local copies, waits for them, and re-layouts  4.15 us
    reduce_sum x1, other arithmetic, local(): jnp.sum(normalized.astype(jnp.float32) * upstream.astype(jnp.float32), ax...  1.84 us
  transfers between devices with their start and end apart: 1, of which 0 were waited for; matrix products, arithmetic and copies ran while one was open for 2% of the time, Pallas kernels for 0%

commit v1 on v0

v1 whole, which is shorter than its diff:
```python
import functools
import math

import jax
import jax.numpy as jnp
from jax import lax
from jax.experimental import pallas as pl
from jax.experimental.pallas import tpu as pltpu
from jax.sharding import PartitionSpec as P

MESH = pl.DeviceIdType.MESH
LANES = 128
CHUNKS = 4


def signs():
    bits = lax.broadcasted_iota(jnp.int32, (LANES, LANES), 0) & lax.broadcasted_iota(
        jnp.int32, (LANES, LANES), 1
    )
    bits = bits ^ (bits >> 4)
    bits = bits ^ (bits >> 2)
    bits = bits ^ (bits >> 1)
    return (1 - 2 * (bits & 1)).astype(jnp.float32).astype(jnp.bfloat16)


def kernel(
    sizes,
    x_hbm,
    u_hbm,
    order_ref,
    index_ref,
    scale_ref,
    query_ref,
    sketch_ref,
    scores_ref,
    x_ref,
    u_ref,
    grads_ref,
    owned_ref,
    pieces_ref,
    own_tab_ref,
    tabs_ref,
    own_query_f32_ref,
    own_query_ref,
    queries_ref,
    had_ref,
    splat_ref,
    weights_ref,
    rot_ref,
    total_ref,
    score_total_ref,
    in_sem,
    piece_send,
    piece_recv,
    relay_send,
    tab_send,
    tab_recv,
    query_send,
    query_recv,
    local_sem,
):
    n_ex, n_col, n_lay, per_col, k_sel = sizes
    ex, col, lay = lax.axis_index("ex"), lax.axis_index("col"), lax.axis_index("lay")
    examples, tokens, features = x_ref.shape
    rows = examples // n_lay
    in_blocks = features // LANES
    layers = index_ref.shape[0]
    out_blocks = query_ref.shape[1] // LANES
    chunk = examples // CHUNKS
    sibling = col + 1 - 2 * lax.rem(col, 2)
    scale = 1.0 / math.sqrt(float(LANES))

    loads = []
    for i in range(CHUNKS):
        part = pl.ds(i * chunk, chunk)
        pair = [
            pltpu.make_async_copy(x_hbm.at[part], x_ref.at[part], in_sem.at[2 * i]),
            pltpu.make_async_copy(u_hbm.at[part], u_ref.at[part], in_sem.at[2 * i + 1]),
        ]
        for copy in pair:
            copy.start()
        loads.append(pair)

    barrier = pltpu.get_barrier_semaphore()
    for dl in range(n_lay):
        for dc in range(n_col):
            if dl or dc:
                pl.semaphore_signal(
                    barrier,
                    inc=1,
                    device_id={
                        "ex": ex,
                        "col": lax.rem(col + dc, n_col),
                        "lay": lax.rem(lay + dl, n_lay),
                    },
                    device_id_type=MESH,
                )
    for j in range(per_col):
        holder = col * per_col + j
        for other in range(n_col):

            @pl.when(holder != ex)
            def _():
                pl.semaphore_signal(
                    barrier,
                    inc=1,
                    device_id={"ex": holder, "col": other, "lay": lay},
                    device_id_type=MESH,
                )

    had_ref[...] = signs()
    own_tab_ref[...] = jnp.full(own_tab_ref.shape, -1.0, jnp.float32)
    for layer in range(layers):
        own_tab_ref[layer, 0:k_sel, 0:in_blocks] = index_ref[layer].astype(jnp.float32)
        own_tab_ref[layer, k_sel : 2 * k_sel, 0:in_blocks] = scale_ref[layer].astype(jnp.float32)
    for o in range(out_blocks):
        own_query_f32_ref[o : o + 1, :] = query_ref[:, o * LANES : (o + 1) * LANES].astype(
            jnp.float32
        )
    own_query_ref[...] = own_query_f32_ref[...].astype(jnp.bfloat16)

    pl.semaphore_wait(barrier, n_lay * n_col - 1 + n_ex - 1)

    def tab_copy(dc):
        return pltpu.make_async_remote_copy(
            src_ref=own_tab_ref,
            dst_ref=tabs_ref.at[col],
            send_sem=tab_send.at[dc],
            recv_sem=tab_recv.at[col],
            device_id={"ex": ex, "col": lax.rem(col + dc, n_col), "lay": lay},
            device_id_type=MESH,
        )

    tab_copies = [tab_copy(dc) for dc in range(1, n_col)]
    for copy in tab_copies:
        copy.start()

    asker = ex // per_col
    slot = lax.rem(ex, per_col)

    def query_copy(target):
        return pltpu.make_async_remote_copy(
            src_ref=own_query_ref,
            dst_ref=queries_ref.at[slot, col],
            send_sem=query_send.at[target],
            recv_sem=query_recv.at[slot, col],
            device_id={"ex": target, "col": asker, "lay": lay},
            device_id_type=MESH,
        )

    def keep_query():
        return pltpu.make_async_copy(
            own_query_ref, queries_ref.at[slot, col], query_recv.at[slot, col]
        )

    for target in range(n_ex):
        mine = jnp.logical_and(target == ex, asker == col)

        @pl.when(jnp.logical_not(mine))
        def _():
            query_copy(target).start()

        @pl.when(mine)
        def _():
            keep_query().start()

    for i in range(CHUNKS):
        for copy in loads[i]:
            copy.wait()
        part = slice(i * chunk, (i + 1) * chunk)
        grads_ref[part, :] = jnp.sum(
            x_ref[part].astype(jnp.float32) * u_ref[part].astype(jnp.float32), axis=1
        ).astype(jnp.bfloat16)
    chosen = (
        lax.broadcasted_iota(jnp.int32, (examples, examples), 0) == order_ref[...]
    ).astype(jnp.float32)
    chosen = chosen.T.astype(jnp.bfloat16)
    ordered = jnp.dot(chosen, grads_ref[...], preferred_element_type=jnp.float32)
    for owner in range(n_lay):
        owned_ref[owner] = ordered[owner * rows : (owner + 1) * rows].astype(jnp.bfloat16)

    offsets = [
        (dl, dc) for dl in range(n_lay) for dc in range(0, n_col, 2) if dl or dc
    ]
    offsets.sort(key=lambda at: (at[0] != 0) + (at[1] != 0))

    def piece_copy(number, dl, dc):
        to_lay, to_col = lax.rem(lay + dl, n_lay), lax.rem(col + dc, n_col)
        return pltpu.make_async_remote_copy(
            src_ref=owned_ref.at[to_lay],
            dst_ref=pieces_ref.at[lay, col],
            send_sem=piece_send.at[number],
            recv_sem=piece_recv.at[lay, col],
            device_id={"ex": ex, "col": to_col, "lay": to_lay},
            device_id_type=MESH,
        )

    def relay_copy(number, source, at_lay, at_col):
        return pltpu.make_async_remote_copy(
            src_ref=source,
            dst_ref=pieces_ref.at[at_lay, at_col],
            send_sem=relay_send.at[number],
            recv_sem=piece_recv.at[at_lay, at_col],
            device_id={"ex": ex, "col": sibling, "lay": lay},
            device_id_type=MESH,
        )

    def arrive(at_lay, at_col):
        pltpu.make_async_remote_copy(
            src_ref=owned_ref.at[0],
            dst_ref=pieces_ref.at[at_lay, at_col],
            send_sem=relay_send.at[0],
            recv_sem=piece_recv.at[at_lay, at_col],
            device_id={"ex": ex, "col": sibling, "lay": lay},
            device_id_type=MESH,
        ).wait_recv()

    sends = [piece_copy(n, dl, dc) for n, (dl, dc) in enumerate(offsets)]
    for copy in sends:
        copy.start()
    own_relay = relay_copy(len(offsets), owned_ref.at[lay], lay, col)
    own_relay.start()
    sends.append(own_relay)

    tabs_ref[col] = own_tab_ref[...]
    for dc in range(1, n_col):
        source = lax.rem(col + dc, n_col)
        pltpu.make_async_remote_copy(
            src_ref=own_tab_ref,
            dst_ref=tabs_ref.at[source],
            send_sem=tab_send.at[dc],
            recv_sem=tab_recv.at[source],
            device_id={"ex": ex, "col": source, "lay": lay},
            device_id_type=MESH,
        ).wait_recv()

    def table(at_lay, at_col, first, count):
        targets = (first + lax.broadcasted_iota(jnp.int32, (count, LANES), 0)).astype(jnp.float32)
        value = jnp.zeros((count, LANES), jnp.float32)
        for k in range(k_sel):
            index = tabs_ref[at_col, at_lay, k : k + 1, :]
            gain = tabs_ref[at_col, at_lay, k_sel + k : k_sel + k + 1, :]
            value = value + jnp.where(targets == index, gain, 0.0)
        return value

    for at_lay in range(layers):
        for at_col in range(n_col):
            mine = table(at_lay, at_col, col * out_blocks, out_blocks) * scale
            for b in range(in_blocks):
                splat_ref[at_lay, at_col, b] = jnp.broadcast_to(
                    mine[:, b : b + 1], (out_blocks, LANES)
                )

    def rotate(source):
        piece = source[...]
        stacked = jnp.concatenate(
            [piece[:, b * LANES : (b + 1) * LANES] for b in range(in_blocks)], axis=0
        )
        rot_ref[...] = jnp.dot(
            stacked, had_ref[...], preferred_element_type=jnp.float32
        ).reshape(in_blocks, rows, LANES)

    group = 4

    def combine(at_lay, at_col, first, last):
        for o in range(0, out_blocks, group):
            if first:
                sums = [jnp.zeros((rows, LANES), jnp.float32) for _ in range(group)]
            else:
                sums = [total_ref[o + g] for g in range(group)]
            for b in range(in_blocks):
                turned = rot_ref[b]
                for g in range(group):
                    sums[g] = sums[g] + turned * splat_ref[at_lay, at_col, b, o + g : o + g + 1, :]
            for g in range(group):
                if last:
                    sketch_ref[:, (o + g) * LANES : (o + g + 1) * LANES] = sums[g].astype(
                        jnp.bfloat16
                    )
                else:
                    total_ref[o + g] = sums[g]

    def score(at_lay, at_col, first, last):
        for q in range(per_col):
            if first:
                sums = jnp.zeros((rows, LANES), jnp.float32)
            else:
                sums = score_total_ref[q]
            for b in range(in_blocks):
                sums = sums + rot_ref[b] * weights_ref[
                    at_lay, at_col, b : b + 1, q * LANES : (q + 1) * LANES
                ]
            if last:
                scores_ref[:, q : q + 1] = jnp.sum(sums, axis=1, keepdims=True) * scale
            else:
                score_total_ref[q] = sums

    rotate(owned_ref.at[lay])
    combine(lay, col, True, False)

    for j in range(per_col):
        holder = col * per_col + j
        for other in range(n_col):
            here = jnp.logical_and(holder == ex, other == col)

            @pl.when(jnp.logical_not(here))
            def _():
                pltpu.make_async_remote_copy(
                    src_ref=own_query_ref,
                    dst_ref=queries_ref.at[j, other],
                    send_sem=query_send.at[0],
                    recv_sem=query_recv.at[j, other],
                    device_id={"ex": holder, "col": other, "lay": lay},
                    device_id_type=MESH,
                ).wait_recv()

            @pl.when(here)
            def _():
                keep_query().wait()

    asked = jnp.concatenate(
        [
            queries_ref[j].astype(jnp.float32).reshape(n_col * out_blocks, LANES)
            for j in range(per_col)
        ],
        axis=1,
    ).astype(jnp.bfloat16)
    for at_lay in range(layers):
        for at_col in range(n_col):
            whole = table(at_lay, at_col, 0, n_col * out_blocks).T.astype(jnp.bfloat16)
            weights_ref[at_lay, at_col] = jnp.dot(
                whole[0 : weights_ref.shape[2]], asked, preferred_element_type=jnp.float32
            )
    score(lay, col, True, False)

    arrive(lay, sibling)
    rotate(pieces_ref.at[lay, sibling])
    combine(lay, sibling, False, False)
    score(lay, sibling, False, False)
    relays = []
    for number, (dl, dc) in enumerate(offsets):
        at_lay, at_col = lax.rem(lay + dl, n_lay), lax.rem(col + dc, n_col)
        arrive(at_lay, at_col)
        relay = relay_copy(number, pieces_ref.at[at_lay, at_col], at_lay, at_col)
        relay.start()
        relays.append(relay)
        rotate(pieces_ref.at[at_lay, at_col])
        combine(at_lay, at_col, False, False)
        score(at_lay, at_col, False, False)
    for number, (dl, dc) in enumerate(offsets):
        at_lay, at_col = lax.rem(lay + dl, n_lay), lax.rem(sibling + dc, n_col)
        last = number == len(offsets) - 1
        arrive(at_lay, at_col)
        rotate(pieces_ref.at[at_lay, at_col])
        combine(at_lay, at_col, False, last)
        score(at_lay, at_col, False, last)

    for copy in sends + relays + tab_copies:
        copy.wait_send()
    for target in range(n_ex):
        mine = jnp.logical_and(target == ex, asker == col)

        @pl.when(jnp.logical_not(mine))
        def _():
            query_copy(target).wait_send()


def solution(mesh):
    n_ex, n_col, n_lay = (mesh.shape[name] for name in ("ex", "col", "lay"))

    def local(normalized, upstream, owner_order, sketch_index, sketch_scale, query_sketch):
        examples, own_layers, tokens, features = normalized.shape
        assert own_layers == 1
        layers, in_blocks, k_sel = sketch_index.shape
        width = query_sketch.shape[1]
        out_blocks = width // LANES
        per_col = n_ex * query_sketch.shape[0] // n_col
        rows = examples // n_lay
        padded = -(-in_blocks // 8) * 8
        vmem = pl.BlockSpec(memory_space=pltpu.VMEM)
        dma = pltpu.SemaphoreType.DMA
        return pl.pallas_call(
            functools.partial(kernel, (n_ex, n_col, n_lay, per_col, k_sel)),
            out_shape=(
                jax.ShapeDtypeStruct((rows, width), jnp.bfloat16),
                jax.ShapeDtypeStruct((rows, per_col), jnp.float32),
            ),
            in_specs=[pl.BlockSpec(memory_space=pl.ANY)] * 2 + [vmem] * 4,
            out_specs=(vmem, vmem),
            scratch_shapes=[
                pltpu.VMEM((examples, tokens, features), jnp.bfloat16),
                pltpu.VMEM((examples, tokens, features), jnp.bfloat16),
                pltpu.VMEM((examples, features), jnp.bfloat16),
                pltpu.VMEM((n_lay, rows, features), jnp.bfloat16),
                pltpu.VMEM((n_lay, n_col, rows, features), jnp.bfloat16),
                pltpu.VMEM((layers, 2 * k_sel, LANES), jnp.float32),
                pltpu.VMEM((n_col, layers, 2 * k_sel, LANES), jnp.float32),
                pltpu.VMEM((out_blocks, LANES), jnp.float32),
                pltpu.VMEM((out_blocks, LANES), jnp.bfloat16),
                pltpu.VMEM((per_col, n_col, out_blocks, LANES), jnp.bfloat16),
                pltpu.VMEM((LANES, LANES), jnp.bfloat16),
                pltpu.VMEM((layers, n_col, in_blocks, out_blocks, LANES), jnp.float32),
                pltpu.VMEM((layers, n_col, padded, per_col * LANES), jnp.float32),
                pltpu.VMEM((in_blocks, rows, LANES), jnp.float32),
                pltpu.VMEM((out_blocks, rows, LANES), jnp.float32),
                pltpu.VMEM((per_col, rows, LANES), jnp.float32),
                dma((2 * CHUNKS,)),
                dma((n_lay * n_col,)),
                dma((n_lay, n_col)),
                dma((n_lay * n_col,)),
                dma((n_col,)),
                dma((n_col,)),
                dma((n_ex,)),
                dma((per_col, n_col)),
                dma((1,)),
            ],
            compiler_params=pltpu.CompilerParams(collective_id=0, has_side_effects=True),
        )(
            normalized.reshape(examples, tokens, features),
            upstream.reshape(examples, tokens, features),
            owner_order,
            jnp.swapaxes(sketch_index, 1, 2),
            jnp.swapaxes(sketch_scale, 1, 2),
            query_sketch,
        )

    placed = (
        P("ex", "lay", None, "col"),
        P("ex", "lay", None, "col"),
        P("ex", None),
        P(None, "col", None),
        P(None, "col", None),
        P("ex", "col"),
    )
    return jax.shard_map(
        local,
        mesh=mesh,
        in_specs=placed,
        out_specs=(P(("ex", "lay"), "col"), P(("ex", "lay"), "col")),
        check_vma=False,
    )
```

time: 54.3 us -> 18.8 us (0.35)
  blocking collectives: 37.8 us -> 0 us
  Pallas kernels: 0 us -> 15 us
  starting transfers between devices: 4.37 us -> 0 us
  other arithmetic: 3.53 us -> 0 us
  local copies, waits for them, and re-layouts: 6.38 us -> 2.87 us
  matrix products: 1.03 us -> 0 us
    all_gather x4 -> x0, blocking collectives: 31.2 us -> none  [the longest x1 13.5 us: local(): lax.all_gather(query_sketch, 'ex', axis=0, tiled=True)]
    pallas_call x0 -> x1, Pallas kernels: none -> 15 us  [local(): pl.pallas_call(functools.partial(kernel, (n_ex, n_col, n_lay, per_col, k_...]
    unnamed x1 -> x0, blocking collectives: 6.58 us -> none
    all_to_all x1 -> x0, starting transfers between devices: 4.37 us -> none  [local(): lax.all_to_all(reordered, 'lay', split_axis=0, concat_axis=1, tiled=True)]
    unnamed x20 -> x1, local copies, waits for them, and re-layouts: 4.15 us -> 1.57 us
    reduce_sum x2 -> x0, other arithmetic: 2.03 us -> none  [the longest x1 1.84 us: local(): jnp.sum(normalized.astype(jnp.float32) * upstream.astype(jnp.float32), ax...]
    select_n x3 -> x0, other arithmetic: 1.48 us -> none  [local(): reordered = jnp.take(local_grads, owner_order[0], axis=0)]
    pallas_call x0 -> x1, local copies, waits for them, and re-layouts: none -> 1.3 us  [local(): pl.pallas_call(functools.partial(kernel, (n_ex, n_col, n_lay, per_col, k_...]
  transfers between devices with their start and end apart: 1 -> 0, of which waited for: 0 -> 0; matrix products, arithmetic and copies ran while one was open for 2% -> 0% of each run, Pallas kernels for 0% -> 0%
where the time goes in v1:
time: 18.8 us; the launch traced here: 18.5 us
  Pallas kernels  15 us (80%)
  local copies, waits for them, and re-layouts  2.87 us (15%)
  between operations  0.64 us (3%)
    pallas_call x1, Pallas kernels, local(): pl.pallas_call(functools.partial(kernel, (n_ex, n_col, n_lay, per_col, k_...  15 us
    unnamed x1, local copies, waits for them, and re-layouts  1.57 us
    pallas_call x1, local copies, waits for them, and re-layouts, local(): pl.pallas_call(functools.partial(kernel, (n_ex, n_col, n_lay, per_col, k_...  1.3 us

profile of v1, /device:TPU:0, one launch (start us, length us, event | category | flops | bytes accessed | tf_op | source)
XLA Modules:
  0.0 18.5 jit_solution(3417404172288878997)
XLA Ops:
  0.6 15.0 %shard_map.77 = (bf16[32,2048]{1,0:T(8,128)(2,1)}, f32[32,1]{1,0:T(8,128)}) custom-call(bf16[64,4,896]{2,1,0:T(4,128)(2,1)} %bitcast.4, bf16[64,4,896]{2,1,0:T(4,128)(2,1)} %bitcast.5, s32[1,64]{1,0:T(1,128)} %order_ref.1, s32[2,4,7]{2,1,0:T(4,128)} %bitcast.6, bf16[2,4,7]{2,1,0:T(4,128)(2,1)} %bitcast.7, bf16[1,2048]{1,0:T(2,128)(2,1)} %query_ref.1), custom_call_target="tpu_custom_call" | custom-call | tf_op jit(solution)/shard_map/pallas_call | solution.py:382
  15.6 1.3 %copy.8 = f32[32,1]{0,1:T(1,128)} copy(f32[32,1]{1,0:T(8,128)} %get-tuple-element.3) | data formatting | bytes 256 | tf_op jit(solution)/shard_map/pallas_call | solution.py:382
  16.9 1.6 %copy.10 = bf16[32,2048]{1,0:T(8,128)(2,1)} copy(bf16[32,2048]{1,0:T(8,128)(2,1)} %get-tuple-element.6) | data formatting | bytes 262144

commit v2 on v1

--- a/solution.py
+++ b/solution.py
@@ -27,12 +27,16 @@
     sizes,
     x_hbm,
     u_hbm,
+    order_hbm,
+    index_hbm,
+    scale_hbm,
+    query_hbm,
+    sketch_ref,
+    scores_ref,
     order_ref,
     index_ref,
     scale_ref,
     query_ref,
-    sketch_ref,
-    scores_ref,
     x_ref,
     u_ref,
     grads_ref,
@@ -50,6 +54,7 @@
     total_ref,
     score_total_ref,
     in_sem,
+    small_sem,
     piece_send,
     piece_recv,
     relay_send,
@@ -81,6 +86,20 @@
             copy.start()
         loads.append(pair)
 
+    smalls = [
+        pltpu.make_async_copy(source, held, small_sem.at[i])
+        for i, (source, held) in enumerate(
+            [
+                (query_hbm, query_ref),
+                (index_hbm, index_ref),
+                (scale_hbm, scale_ref),
+                (order_hbm, order_ref),
+            ]
+        )
+    ]
+    for copy in smalls:
+        copy.start()
+
     barrier = pltpu.get_barrier_semaphore()
     for dl in range(n_lay):
         for dc in range(n_col):
@@ -109,6 +128,8 @@
                 )
 
     had_ref[...] = signs()
+    for copy in smalls:
+        copy.wait()
     own_tab_ref[...] = jnp.full(own_tab_ref.shape, -1.0, jnp.float32)
     for layer in range(layers):
         own_tab_ref[layer, 0:k_sel, 0:in_blocks] = index_ref[layer].astype(jnp.float32)
@@ -118,51 +139,6 @@
             jnp.float32
         )
     own_query_ref[...] = own_query_f32_ref[...].astype(jnp.bfloat16)
-
-    pl.semaphore_wait(barrier, n_lay * n_col - 1 + n_ex - 1)
-
-    def tab_copy(dc):
-        return pltpu.make_async_remote_copy(
-            src_ref=own_tab_ref,
-            dst_ref=tabs_ref.at[col],
-            send_sem=tab_send.at[dc],
-            recv_sem=tab_recv.at[col],
-            device_id={"ex": ex, "col": lax.rem(col + dc, n_col), "lay": lay},
-            device_id_type=MESH,
-        )
-
-    tab_copies = [tab_copy(dc) for dc in range(1, n_col)]
-    for copy in tab_copies:
-        copy.start()
-
-    asker = ex // per_col
-    slot = lax.rem(ex, per_col)
-
-    def query_copy(target):
-        return pltpu.make_async_remote_copy(
-            src_ref=own_query_ref,
-            dst_ref=queries_ref.at[slot, col],
-            send_sem=query_send.at[target],
-            recv_sem=query_recv.at[slot, col],
-            device_id={"ex": target, "col": asker, "lay": lay},
-            device_id_type=MESH,
-        )
-
-    def keep_query():
-        return pltpu.make_async_copy(
-            own_query_ref, queries_ref.at[slot, col], query_recv.at[slot, col]
-        )
-
-    for target in range(n_ex):
-        mine = jnp.logical_and(target == ex, asker == col)
-
-        @pl.when(jnp.logical_not(mine))
-        def _():
-            query_copy(target).start()
-
-        @pl.when(mine)
-        def _():
-            keep_query().start()
 
     for i in range(CHUNKS):
         for copy in loads[i]:
@@ -178,6 +154,51 @@
     ordered = jnp.dot(chosen, grads_ref[...], preferred_element_type=jnp.float32)
     for owner in range(n_lay):
         owned_ref[owner] = ordered[owner * rows : (owner + 1) * rows].astype(jnp.bfloat16)
+
+    pl.semaphore_wait(barrier, n_lay * n_col - 1 + n_ex - 1)
+
+    def tab_copy(dc):
+        return pltpu.make_async_remote_copy(
+            src_ref=own_tab_ref,
+            dst_ref=tabs_ref.at[col],
+            send_sem=tab_send.at[dc],
+            recv_sem=tab_recv.at[col],
+            device_id={"ex": ex, "col": lax.rem(col + dc, n_col), "lay": lay},
+            device_id_type=MESH,
+        )
+
+    tab_copies = [tab_copy(dc) for dc in range(1, n_col)]
+    for copy in tab_copies:
+        copy.start()
+
+    asker = ex // per_col
+    slot = lax.rem(ex, per_col)
+
+    def query_copy(target):
+        return pltpu.make_async_remote_copy(
+            src_ref=own_query_ref,
+            dst_ref=queries_ref.at[slot, col],
+            send_sem=query_send.at[target],
+            recv_sem=query_recv.at[slot, col],
+            device_id={"ex": target, "col": asker, "lay": lay},
+            device_id_type=MESH,
+        )
+
+    def keep_query():
+        return pltpu.make_async_copy(
+            own_query_ref, queries_ref.at[slot, col], query_recv.at[slot, col]
+        )
+
+    for target in range(n_ex):
+        mine = jnp.logical_and(target == ex, asker == col)
+
+        @pl.when(jnp.logical_not(mine))
+        def _():
+            query_copy(target).start()
+
+        @pl.when(mine)
+        def _():
+            keep_query().start()
 
     offsets = [
         (dl, dc) for dl in range(n_lay) for dc in range(0, n_col, 2) if dl or dc
@@ -291,7 +312,7 @@
                     at_lay, at_col, b : b + 1, q * LANES : (q + 1) * LANES
                 ]
             if last:
-                scores_ref[:, q : q + 1] = jnp.sum(sums, axis=1, keepdims=True) * scale
+                scores_ref[q : q + 1, :] = jnp.sum(sums.T, axis=0, keepdims=True) * scale
             else:
                 score_total_ref[q] = sums
 
@@ -379,15 +400,19 @@
         padded = -(-in_blocks // 8) * 8
         vmem = pl.BlockSpec(memory_space=pltpu.VMEM)
         dma = pltpu.SemaphoreType.DMA
-        return pl.pallas_call(
+        sketch, scores = pl.pallas_call(
             functools.partial(kernel, (n_ex, n_col, n_lay, per_col, k_sel)),
             out_shape=(
-                jax.ShapeDtypeStruct((rows, width), jnp.bfloat16),
-                jax.ShapeDtypeStruct((rows, per_col), jnp.float32),
+                pltpu.VMEM((rows, width), jnp.bfloat16),
+                pltpu.VMEM((per_col, rows), jnp.float32),
             ),
-            in_specs=[pl.BlockSpec(memory_space=pl.ANY)] * 2 + [vmem] * 4,
+            in_specs=[pl.BlockSpec(memory_space=pl.ANY)] * 6,
             out_specs=(vmem, vmem),
             scratch_shapes=[
+                pltpu.VMEM(owner_order.shape, jnp.int32),
+                pltpu.VMEM((layers, k_sel, in_blocks), jnp.int32),
+                pltpu.VMEM((layers, k_sel, in_blocks), jnp.bfloat16),
+                pltpu.VMEM(query_sketch.shape, jnp.bfloat16),
                 pltpu.VMEM((examples, tokens, features), jnp.bfloat16),
                 pltpu.VMEM((examples, tokens, features), jnp.bfloat16),
                 pltpu.VMEM((examples, features), jnp.bfloat16),
@@ -405,6 +430,7 @@
                 pltpu.VMEM((out_blocks, rows, LANES), jnp.float32),
                 pltpu.VMEM((per_col, rows, LANES), jnp.float32),
                 dma((2 * CHUNKS,)),
+                dma((4,)),
                 dma((n_lay * n_col,)),
                 dma((n_lay, n_col)),
                 dma((n_lay * n_col,)),
@@ -423,6 +449,7 @@
             jnp.swapaxes(sketch_scale, 1, 2),
             query_sketch,
         )
+        return sketch, scores.T
 
     placed = (
         P("ex", "lay", None, "col"),

time: 18.8 us -> 14.8 us (0.79)
  Pallas kernels: 15 us -> 12.9 us
  local copies, waits for them, and re-layouts: 2.87 us -> 1.17 us
    pallas_call x1, Pallas kernels: 15 us -> 12.9 us  [local(): pl.pallas_call(functools.partial(kernel, (n_ex, n_col, n_lay, per_col, k_...]
    pallas_call x1 -> x0, local copies, waits for them, and re-layouts: 1.3 us -> none  [local(): pl.pallas_call(functools.partial(kernel, (n_ex, n_col, n_lay, per_col, k_...]
    unnamed x1 -> x2, local copies, waits for them, and re-layouts: 1.57 us -> 1.17 us
where the time goes in v2:
time: 14.8 us; the launch traced here: 14.7 us
  Pallas kernels  12.9 us (87%)
  local copies, waits for them, and re-layouts  1.17 us (8%)
  between operations  0.64 us (4%)
    pallas_call x1, Pallas kernels, local(): pl.pallas_call(functools.partial(kernel, (n_ex, n_col, n_lay, per_col, k_...  12.9 us
    unnamed x2, local copies, waits for them, and re-layouts  1.17 us

profile of v2, /device:TPU:0, one launch (start us, length us, event | category | flops | bytes accessed | tf_op | source)
XLA Modules:
  0.0 14.7 jit_solution(7210086187711351470)
XLA Ops:
  0.6 12.9 %shard_map.77 = (bf16[32,2048]{1,0:T(8,128)(2,1)S(1)}, f32[1,32]{1,0:T(1,128)S(1)}) custom-call(bf16[64,4,896]{2,1,0:T(4,128)(2,1)} %bitcast.6, bf16[64,4,896]{2,1,0:T(4,128)(2,1)} %bitcast.7, s32[1,64]{1,0:T(1,128)} %order_hbm.1, s32[2,4,7]{2,1,0:T(4,128)} %bitcast.8, bf16[2,4,7]{2,1,0:T(4,128)(2,1)} %bitcast.9, bf16[1,2048]{1,0:T(2,128)(2,1)} %query_hbm.1), custom_call_target="tpu_custom_call" | custom-call | tf_op jit(solution)/shard_map/pallas_call | solution.py:403
  13.5 0.7 %copy.10 = bf16[32,2048]{1,0:T(8,128)(2,1)} copy(bf16[32,2048]{1,0:T(8,128)(2,1)S(1)} %get-tuple-element.6) | data formatting | bytes 262144
  14.1 0.5 %copy.11 = f32[32,1]{0,1:T(1,128)} copy(f32[32,1]{0,1:T(1,128)S(1)} %bitcast.5) | data formatting | bytes 256

commit v3 on v2

--- a/solution.py
+++ b/solution.py
@@ -49,10 +49,10 @@
     queries_ref,
     had_ref,
     splat_ref,
+    turned_tab_ref,
     weights_ref,
     rot_ref,
     total_ref,
-    score_total_ref,
     in_sem,
     small_sem,
     piece_send,
@@ -62,7 +62,7 @@
     tab_recv,
     query_send,
     query_recv,
-    local_sem,
+    ready_sem,
 ):
     n_ex, n_col, n_lay, per_col, k_sel = sizes
     ex, col, lay = lax.axis_index("ex"), lax.axis_index("col"), lax.axis_index("lay")
@@ -71,6 +71,7 @@
     in_blocks = features // LANES
     layers = index_ref.shape[0]
     out_blocks = query_ref.shape[1] // LANES
+    padded = weights_ref.shape[2]
     chunk = examples // CHUNKS
     sibling = col + 1 - 2 * lax.rem(col, 2)
     scale = 1.0 / math.sqrt(float(LANES))
@@ -114,18 +115,18 @@
                     },
                     device_id_type=MESH,
                 )
-    for j in range(per_col):
-        holder = col * per_col + j
-        for other in range(n_col):
-
-            @pl.when(holder != ex)
-            def _():
-                pl.semaphore_signal(
-                    barrier,
-                    inc=1,
-                    device_id={"ex": holder, "col": other, "lay": lay},
-                    device_id_type=MESH,
-                )
+    has_lower, has_upper = ex > 0, ex < n_ex - 1
+
+    def signal_plane(sem, step):
+        pl.semaphore_signal(
+            sem,
+            inc=1,
+            device_id={"ex": ex + step, "col": col, "lay": lay},
+            device_id_type=MESH,
+        )
+
+    pl.when(has_lower)(lambda: signal_plane(barrier, -1))
+    pl.when(has_upper)(lambda: signal_plane(barrier, 1))
 
     had_ref[...] = signs()
     for copy in smalls:
@@ -155,7 +156,10 @@
     for owner in range(n_lay):
         owned_ref[owner] = ordered[owner * rows : (owner + 1) * rows].astype(jnp.bfloat16)
 
-    pl.semaphore_wait(barrier, n_lay * n_col - 1 + n_ex - 1)
+    planes = has_lower.astype(jnp.int32) + has_upper.astype(jnp.int32)
+    pl.semaphore_wait(barrier, n_lay * n_col - 1 + planes)
+    pl.when(jnp.logical_not(has_lower))(lambda: signal_plane(ready_sem.at[0], 1))
+    pl.when(jnp.logical_not(has_upper))(lambda: signal_plane(ready_sem.at[1], -1))
 
     def tab_copy(dc):
         return pltpu.make_async_remote_copy(
@@ -189,16 +193,34 @@
             own_query_ref, queries_ref.at[slot, col], query_recv.at[slot, col]
         )
 
-    for target in range(n_ex):
+    def send_query(target, wanted):
         mine = jnp.logical_and(target == ex, asker == col)
 
-        @pl.when(jnp.logical_not(mine))
+        @pl.when(jnp.logical_and(wanted, jnp.logical_not(mine)))
         def _():
             query_copy(target).start()
 
-        @pl.when(mine)
+        @pl.when(jnp.logical_and(wanted, mine))
         def _():
             keep_query().start()
+
+    def lower_planes():
+        @pl.when(has_lower)
+        def _():
+            pl.semaphore_wait(ready_sem.at[0], 1)
+            pl.when(has_upper)(lambda: signal_plane(ready_sem.at[0], 1))
+
+        for target in range(n_ex):
+            send_query(target, target <= ex)
+
+    def upper_planes(here):
+        @pl.when(jnp.logical_and(here, has_upper))
+        def _():
+            pl.semaphore_wait(ready_sem.at[1], 1)
+            pl.when(has_lower)(lambda: signal_plane(ready_sem.at[1], -1))
+
+        for target in range(n_ex):
+            send_query(target, jnp.logical_and(here, target > ex))
 
     offsets = [
         (dl, dc) for dl in range(n_lay) for dc in range(0, n_col, 2) if dl or dc
@@ -242,6 +264,8 @@
     own_relay = relay_copy(len(offsets), owned_ref.at[lay], lay, col)
     own_relay.start()
     sends.append(own_relay)
+
+    lower_planes()
 
     tabs_ref[col] = own_tab_ref[...]
     for dc in range(1, n_col):
@@ -272,12 +296,12 @@
                     mine[:, b : b + 1], (out_blocks, LANES)
                 )
 
-    def rotate(source):
+    def rotate(source, at_lay, at_col):
         piece = source[...]
         stacked = jnp.concatenate(
             [piece[:, b * LANES : (b + 1) * LANES] for b in range(in_blocks)], axis=0
         )
-        rot_ref[...] = jnp.dot(
+        rot_ref[at_lay, at_col] = jnp.dot(
             stacked, had_ref[...], preferred_element_type=jnp.float32
         ).reshape(in_blocks, rows, LANES)
 
@@ -290,7 +314,7 @@
             else:
                 sums = [total_ref[o + g] for g in range(group)]
             for b in range(in_blocks):
-                turned = rot_ref[b]
+                turned = rot_ref[at_lay, at_col, b]
                 for g in range(group):
                     sums[g] = sums[g] + turned * splat_ref[at_lay, at_col, b, o + g : o + g + 1, :]
             for g in range(group):
@@ -301,23 +325,35 @@
                 else:
                     total_ref[o + g] = sums[g]
 
-    def score(at_lay, at_col, first, last):
-        for q in range(per_col):
-            if first:
-                sums = jnp.zeros((rows, LANES), jnp.float32)
-            else:
-                sums = score_total_ref[q]
-            for b in range(in_blocks):
-                sums = sums + rot_ref[b] * weights_ref[
-                    at_lay, at_col, b : b + 1, q * LANES : (q + 1) * LANES
-                ]
-            if last:
-                scores_ref[q : q + 1, :] = jnp.sum(sums.T, axis=0, keepdims=True) * scale
-            else:
-                score_total_ref[q] = sums
-
-    rotate(owned_ref.at[lay])
+    rotate(owned_ref.at[lay], lay, col)
     combine(lay, col, True, False)
+
+    for at_lay in range(layers):
+        for at_col in range(n_col):
+            whole = table(at_lay, at_col, 0, n_col * out_blocks).T
+            turned_tab_ref[at_lay, at_col] = whole[0:padded].astype(jnp.bfloat16)
+
+    arrive(lay, sibling)
+    rotate(pieces_ref.at[lay, sibling], lay, sibling)
+    combine(lay, sibling, False, False)
+    upper_planes(has_lower)
+    relays = []
+    for number, (dl, dc) in enumerate(offsets):
+        if number == len(offsets) - 1:
+            upper_planes(jnp.logical_not(has_lower))
+        at_lay, at_col = lax.rem(lay + dl, n_lay), lax.rem(col + dc, n_col)
+        arrive(at_lay, at_col)
+        relay = relay_copy(number, pieces_ref.at[at_lay, at_col], at_lay, at_col)
+        relay.start()
+        relays.append(relay)
+        rotate(pieces_ref.at[at_lay, at_col], at_lay, at_col)
+        combine(at_lay, at_col, False, False)
+    for number, (dl, dc) in enumerate(offsets):
+        at_lay, at_col = lax.rem(lay + dl, n_lay), lax.rem(sibling + dc, n_col)
+        last = number == len(offsets) - 1
+        arrive(at_lay, at_col)
+        rotate(pieces_ref.at[at_lay, at_col], at_lay, at_col)
+        combine(at_lay, at_col, False, last)
 
     for j in range(per_col):
         holder = col * per_col + j
@@ -346,35 +382,20 @@
         ],
         axis=1,
     ).astype(jnp.bfloat16)
-    for at_lay in range(layers):
-        for at_col in range(n_col):
-            whole = table(at_lay, at_col, 0, n_col * out_blocks).T.astype(jnp.bfloat16)
-            weights_ref[at_lay, at_col] = jnp.dot(
-                whole[0 : weights_ref.shape[2]], asked, preferred_element_type=jnp.float32
-            )
-    score(lay, col, True, False)
-
-    arrive(lay, sibling)
-    rotate(pieces_ref.at[lay, sibling])
-    combine(lay, sibling, False, False)
-    score(lay, sibling, False, False)
-    relays = []
-    for number, (dl, dc) in enumerate(offsets):
-        at_lay, at_col = lax.rem(lay + dl, n_lay), lax.rem(col + dc, n_col)
-        arrive(at_lay, at_col)
-        relay = relay_copy(number, pieces_ref.at[at_lay, at_col], at_lay, at_col)
-        relay.start()
-        relays.append(relay)
-        rotate(pieces_ref.at[at_lay, at_col])
-        combine(at_lay, at_col, False, False)
-        score(at_lay, at_col, False, False)
-    for number, (dl, dc) in enumerate(offsets):
-        at_lay, at_col = lax.rem(lay + dl, n_lay), lax.rem(sibling + dc, n_col)
-        last = number == len(offsets) - 1
-        arrive(at_lay, at_col)
-        rotate(pieces_ref.at[at_lay, at_col])
-        combine(at_lay, at_col, False, last)
-        score(at_lay, at_col, False, last)
+    weights_ref[...] = jnp.dot(
+        turned_tab_ref[...].reshape(layers * n_col * padded, n_col * out_blocks),
+        asked,
+        preferred_element_type=jnp.float32,
+    ).reshape(weights_ref.shape)
+    for q in range(per_col):
+        sums = jnp.zeros((rows, LANES), jnp.float32)
+        for at_lay in range(layers):
+            for at_col in range(n_col):
+                for b in range(in_blocks):
+                    sums = sums + rot_ref[at_lay, at_col, b] * weights_ref[
+                        at_lay, at_col, b : b + 1, q * LANES : (q + 1) * LANES
+                    ]
+        scores_ref[q : q + 1, :] = jnp.sum(sums.T, axis=0, keepdims=True) * scale
 
     for copy in sends + relays + tab_copies:
         copy.wait_send()
@@ -397,7 +418,7 @@
         out_blocks = width // LANES
         per_col = n_ex * query_sketch.shape[0] // n_col
         rows = examples // n_lay
-        padded = -(-in_blocks // 8) * 8
+        padded = -(-in_blocks // 16) * 16
         vmem = pl.BlockSpec(memory_space=pltpu.VMEM)
         dma = pltpu.SemaphoreType.DMA
         sketch, scores = pl.pallas_call(
@@ -425,10 +446,10 @@
                 pltpu.VMEM((per_col, n_col, out_blocks, LANES), jnp.bfloat16),
                 pltpu.VMEM((LANES, LANES), jnp.bfloat16),
                 pltpu.VMEM((layers, n_col, in_blocks, out_blocks, LANES), jnp.float32),
+                pltpu.VMEM((layers, n_col, padded, n_col * out_blocks), jnp.bfloat16),
                 pltpu.VMEM((layers, n_col, padded, per_col * LANES), jnp.float32),
-                pltpu.VMEM((in_blocks, rows, LANES), jnp.float32),
+                pltpu.VMEM((n_lay, n_col, in_blocks, rows, LANES), jnp.float32),
                 pltpu.VMEM((out_blocks, rows, LANES), jnp.float32),
-                pltpu.VMEM((per_col, rows, LANES), jnp.float32),
                 dma((2 * CHUNKS,)),
                 dma((4,)),
                 dma((n_lay * n_col,)),
@@ -438,7 +459,7 @@
                 dma((n_col,)),
                 dma((n_ex,)),
                 dma((per_col, n_col)),
-                dma((1,)),
+                pltpu.SemaphoreType.REGULAR((2,)),
             ],
             compiler_params=pltpu.CompilerParams(collective_id=0, has_side_effects=True),
         )(

time: 14.8 us -> 14.4 us (0.973)
  Pallas kernels: 12.9 us -> 12.4 us
    pallas_call x1, Pallas kernels: 12.9 us -> 12.4 us  [local(): pl.pallas_call(functools.partial(kernel, (n_ex, n_col, n_lay, per_col, k_...]
where the time goes in v3:
time: 14.4 us; the launch traced here: 14.2 us
  Pallas kernels  12.4 us (86%)
  local copies, waits for them, and re-layouts  1.17 us (8%)
  between operations  0.64 us (4%)
    pallas_call x1, Pallas kernels, local(): pl.pallas_call(functools.partial(kernel, (n_ex, n_col, n_lay, per_col, k_...  12.4 us
    unnamed x2, local copies, waits for them, and re-layouts  1.17 us

profile of v3, /device:TPU:0, one launch (start us, length us, event | category | flops | bytes accessed | tf_op | source)
XLA Modules:
  0.0 14.2 jit_solution(5890677249681366283)
XLA Ops:
  0.6 12.4 %shard_map.77 = (bf16[32,2048]{1,0:T(8,128)(2,1)S(1)}, f32[1,32]{1,0:T(1,128)S(1)}) custom-call(bf16[64,4,896]{2,1,0:T(4,128)(2,1)} %bitcast.6, bf16[64,4,896]{2,1,0:T(4,128)(2,1)} %bitcast.7, s32[1,64]{1,0:T(1,128)} %order_hbm.1, s32[2,4,7]{2,1,0:T(4,128)} %bitcast.8, bf16[2,4,7]{2,1,0:T(4,128)(2,1)} %bitcast.9, bf16[1,2048]{1,0:T(2,128)(2,1)} %query_hbm.1), custom_call_target="tpu_custom_call" | custom-call | tf_op jit(solution)/shard_map/pallas_call | solution.py:424
  13.1 0.7 %copy.10 = bf16[32,2048]{1,0:T(8,128)(2,1)} copy(bf16[32,2048]{1,0:T(8,128)(2,1)S(1)} %get-tuple-element.6) | data formatting | bytes 262144
  13.7 0.5 %copy.11 = f32[32,1]{0,1:T(1,128)} copy(f32[32,1]{0,1:T(1,128)S(1)} %bitcast.5) | data formatting | bytes 256

commit v4 on v3

--- a/solution.py
+++ b/solution.py
@@ -141,7 +141,26 @@
         )
     own_query_ref[...] = own_query_f32_ref[...].astype(jnp.bfloat16)
 
+    def tab_copy(dc):
+        return pltpu.make_async_remote_copy(
+            src_ref=own_tab_ref,
+            dst_ref=tabs_ref.at[col],
+            send_sem=tab_send.at[dc],
+            recv_sem=tab_recv.at[col],
+            device_id={"ex": ex, "col": lax.rem(col + dc, n_col), "lay": lay},
+            device_id_type=MESH,
+        )
+
     for i in range(CHUNKS):
+        if i == CHUNKS // 2:
+            planes = has_lower.astype(jnp.int32) + has_upper.astype(jnp.int32)
+            pl.semaphore_wait(barrier, n_lay * n_col - 1 + planes)
+            pl.when(jnp.logical_not(has_lower))(lambda: signal_plane(ready_sem.at[0], 1))
+            pl.when(jnp.logical_not(has_upper))(lambda: signal_plane(ready_sem.at[1], -1))
+            tab_copies = [tab_copy(dc) for dc in range(1, n_col)]
+            for copy in tab_copies:
+                copy.start()
+
         for copy in loads[i]:
             copy.wait()
         part = slice(i * chunk, (i + 1) * chunk)
@@ -156,25 +175,6 @@
     for owner in range(n_lay):
         owned_ref[owner] = ordered[owner * rows : (owner + 1) * rows].astype(jnp.bfloat16)
 
-    planes = has_lower.astype(jnp.int32) + has_upper.astype(jnp.int32)
-    pl.semaphore_wait(barrier, n_lay * n_col - 1 + planes)
-    pl.when(jnp.logical_not(has_lower))(lambda: signal_plane(ready_sem.at[0], 1))
-    pl.when(jnp.logical_not(has_upper))(lambda: signal_plane(ready_sem.at[1], -1))
-
-    def tab_copy(dc):
-        return pltpu.make_async_remote_copy(
-            src_ref=own_tab_ref,
-            dst_ref=tabs_ref.at[col],
-            send_sem=tab_send.at[dc],
-            recv_sem=tab_recv.at[col],
-            device_id={"ex": ex, "col": lax.rem(col + dc, n_col), "lay": lay},
-            device_id_type=MESH,
-        )
-
-    tab_copies = [tab_copy(dc) for dc in range(1, n_col)]
-    for copy in tab_copies:
-        copy.start()
-
     asker = ex // per_col
     slot = lax.rem(ex, per_col)
 
@@ -259,13 +259,14 @@
         ).wait_recv()
 
     sends = [piece_copy(n, dl, dc) for n, (dl, dc) in enumerate(offsets)]
-    for copy in sends:
+    for copy in reversed(sends):
         copy.start()
     own_relay = relay_copy(len(offsets), owned_ref.at[lay], lay, col)
     own_relay.start()
     sends.append(own_relay)
 
     lower_planes()
+    upper_planes(has_lower)
 
     tabs_ref[col] = own_tab_ref[...]
     for dc in range(1, n_col):
@@ -336,11 +337,9 @@
     arrive(lay, sibling)
     rotate(pieces_ref.at[lay, sibling], lay, sibling)
     combine(lay, sibling, False, False)
-    upper_planes(has_lower)
+    upper_planes(jnp.logical_not(has_lower))
     relays = []
     for number, (dl, dc) in enumerate(offsets):
-        if number == len(offsets) - 1:
-            upper_planes(jnp.logical_not(has_lower))
         at_lay, at_col = lax.rem(lay + dl, n_lay), lax.rem(col + dc, n_col)
         arrive(at_lay, at_col)
         relay = relay_copy(number, pieces_ref.at[at_lay, at_col], at_lay, at_col)

time: 14.4 us -> 13.3 us (0.924)
  Pallas kernels: 12.4 us -> 11.4 us
    pallas_call x1, Pallas kernels: 12.4 us -> 11.4 us  [local(): pl.pallas_call(functools.partial(kernel, (n_ex, n_col, n_lay, per_col, k_...]
where the time goes in v4:
time: 13.3 us; the launch traced here: 13.2 us
  Pallas kernels  11.4 us (86%)
  local copies, waits for them, and re-layouts  1.17 us (9%)
  between operations  0.64 us (5%)
    pallas_call x1, Pallas kernels, local(): pl.pallas_call(functools.partial(kernel, (n_ex, n_col, n_lay, per_col, k_...  11.4 us
    unnamed x2, local copies, waits for them, and re-layouts  1.17 us

profile of v4, /device:TPU:0, one launch (start us, length us, event | category | flops | bytes accessed | tf_op | source)
XLA Modules:
  0.0 13.2 jit_solution(13419250567807446645)
XLA Ops:
  0.6 11.4 %shard_map.77 = (bf16[32,2048]{1,0:T(8,128)(2,1)S(1)}, f32[1,32]{1,0:T(1,128)S(1)}) custom-call(bf16[64,4,896]{2,1,0:T(4,128)(2,1)} %bitcast.6, bf16[64,4,896]{2,1,0:T(4,128)(2,1)} %bitcast.7, s32[1,64]{1,0:T(1,128)} %order_hbm.1, s32[2,4,7]{2,1,0:T(4,128)} %bitcast.8, bf16[2,4,7]{2,1,0:T(4,128)(2,1)} %bitcast.9, bf16[1,2048]{1,0:T(2,128)(2,1)} %query_hbm.1), custom_call_target="tpu_custom_call" | custom-call | tf_op jit(solution)/shard_map/pallas_call | solution.py:423
  12.0 0.7 %copy.10 = bf16[32,2048]{1,0:T(8,128)(2,1)} copy(bf16[32,2048]{1,0:T(8,128)(2,1)S(1)} %get-tuple-element.6) | data formatting | bytes 262144
  12.7 0.5 %copy.11 = f32[32,1]{0,1:T(1,128)} copy(f32[32,1]{0,1:T(1,128)S(1)} %bitcast.5) | data formatting | bytes 256
